TPU v7x, 32 devices: a whole 2x2x4 slice. The times are simulated.
32 devices in a mesh: lines: 4 (over y, x), buses: 8 (over z, core).
Axes of the slice: x: 2, y: 2, z: 4, core: 2. Of those that a mesh axis runs over, the one named last changes fastest.
Arguments:
- ptdf: bfloat16 [4096, 10240], P('lines', 'buses'), may hold values from -0.078125 to 0.078125
- load: float32 [384, 10240], P(None, 'buses'), may hold values from 0.03 to 3.8, as said below
- ratings: float32 [32768], replicated, may hold values from 0.3 to 3
- line_index: int32 [4096], P('lines'), may hold values from 0 to 32767
- gen_bus: int32 [2048], P('buses'), may hold values from 0 to 10239, as said below
- gen_quad: float32 [2048], P('buses'), may hold values from 0.05 to 0.5
- gen_lin: float32 [2048], P('buses'), may hold values from 0.5 to 2.5
- gen_max: float32 [2048], P('buses'), may hold values from 0.8 to 4
- gen_start: float32 [384, 2048], P(None, 'buses'), may hold values from 0 to 2
- stor_bus: int32 [1024], P('buses'), may hold values from 0 to 1279
- stor_quad: float32 [1024], P('buses'), may hold values from 0.05 to 0.5
- stor_rate: float32 [1024], P('buses'), may hold values from 0.3 to 1.5
- stor_energy: float32 [1024], P('buses'), may hold values from 1 to 8
- stor_start: float32 [384, 1024], P(None, 'buses'), may hold values from -0.5 to 0.5
- lam_start: float32 [384], replicated, may hold values from -4 to 4
- mu_start: float32 [384, 4096], P(None, ('lines', 'buses')), may hold values from -3 to 3
- omega_start: float32 [384, 1024], P(None, 'buses'), may hold values from -2 to 2
Outputs:
- gen_out: float32 [384, 2048], P(None, 'buses')
- stor_out: float32 [384, 1024], P(None, 'buses')
- lam_out: float32 [384], replicated
- mu_out: float32 [384, 4096], P(None, ('lines', 'buses'))
- omega_out: float32 [384, 1024], P(None, 'buses')
Inputs may be any that keep to these rules, and one draw needn't show every extreme that they name: `gen_bus`: of the 256 generators of one area at most 32 sit on the buses of any one area (1280 consecutive buses); in every draw one area holds exactly 32 generators of every area, and the others of an area spread over the remaining areas as evenly as counts allow. `load`: loads are positive.
All inputs are finite; a program needn't handle non-finite values.
Results may differ from a plain program's by a relative error of at most 0.0075.
Values may be sent and summed in bfloat16 or wider, within the bound.
A program may use at most 64 MiB of HBM per device.

v0:
```python
import jax
import jax.numpy as jnp
from jax import lax
from jax.sharding import PartitionSpec as P

HOURS = 24
TAU = 0.25
SIGMA_FLOW = 4.0
SIGMA_STORE = 0.25
KAPPA = 1.0
THETA = 0.5


def reverse_cum(values, hour_count):
    total_rows, columns = values.shape
    shaped = values.reshape(total_rows // hour_count, hour_count, columns)
    summed = jnp.flip(jnp.cumsum(jnp.flip(shaped, 1), axis=1), 1)
    return summed.reshape(total_rows, columns)


def forward_cum(values, hour_count):
    total_rows, columns = values.shape
    shaped = values.reshape(total_rows // hour_count, hour_count, columns)
    return jnp.cumsum(shaped, axis=1).reshape(total_rows, columns)


def dual_step(dual_now, image_term, step_size, low_bound, high_bound):
    shifted = dual_now + step_size * image_term
    return shifted - step_size * jnp.clip(shifted / step_size, low_bound, high_bound)


def shards(
    ptdf,
    load,
    ratings,
    line_index,
    gen_bus,
    gen_quad,
    gen_lin,
    gen_max,
    gen_start,
    stor_bus,
    stor_quad,
    stor_rate,
    stor_energy,
    stor_start,
    lam_start,
    mu_start,
    omega_start,
):
    row_count = load.shape[0]
    line_count, bus_count = ptdf.shape
    gen_count = gen_bus.shape[0]
    stor_count = stor_bus.shape[0]
    device_count = lax.axis_size("buses")
    slot_count = max(8, (gen_count + device_count - 1) // device_count)
    slot_width = device_count * slot_count
    share_len = line_count // device_count
    share_start = lax.axis_index("buses") * share_len
    target = gen_bus // bus_count
    local_bus = gen_bus % bus_count
    target_hit = (target[:, None] == jnp.arange(device_count, dtype=jnp.int32)[None, :]).astype(
        jnp.int32
    )
    rank_in = jnp.sum(target_hit * jnp.cumsum(target_hit, axis=0), axis=1) - 1
    column = target * slot_count + rank_in
    slot_ids = jnp.full((slot_width,), -1, jnp.int32).at[column].set(local_bus)
    arrived = lax.all_to_all(slot_ids[None, :], "buses", split_axis=1, concat_axis=1, tiled=True)
    arrived_bus = jnp.maximum(arrived[0], 0)
    limit_block = jnp.take(ratings, line_index)
    limit_share = lax.dynamic_slice_in_dim(limit_block, share_start, share_len)
    hour_of = jnp.arange(row_count, dtype=jnp.int32) % HOURS
    last_hour = (hour_of == HOURS - 1)[:, None]
    half_energy = (0.5 * stor_energy)[None, :]
    low_bound = jnp.where(last_hour, jnp.zeros_like(half_energy), -half_energy)
    high_bound = jnp.where(last_hour, jnp.zeros_like(half_energy), half_energy)
    load_total = jnp.sum(load, axis=1)
    total_units = (gen_count + stor_count) * device_count
    dual_flow = mu_start
    gen_now, stor_now = (gen_start, stor_start)
    gen_old, stor_old = (gen_start, stor_start)
    price_level, dual_store = (lam_start, omega_start)
    for iteration in range(2):
        if iteration == 0:
            gen_mid, stor_mid = (gen_now, stor_now)
        else:
            gen_mid = gen_now + THETA * (gen_now - gen_old)
            stor_mid = stor_now + THETA * (stor_now - stor_old)
        dual_low = lax.all_gather(dual_flow.astype(jnp.bfloat16), "buses", axis=1, tiled=True)
        partial_value = jnp.dot(dual_low, ptdf, preferred_element_type=jnp.float32)
        bus_price = lax.psum(partial_value.astype(jnp.bfloat16), "lines").astype(jnp.float32)
        gen_part = jnp.take(
            lax.all_to_all(
                jnp.take(bus_price, arrived_bus, axis=1).astype(jnp.bfloat16),
                "buses",
                split_axis=1,
                concat_axis=1,
                tiled=True,
            ).astype(jnp.float32),
            column,
            axis=1,
        )
        stor_price = jnp.take(bus_price, stor_bus, axis=1)
        gen_grad = 2.0 * gen_quad * gen_mid + gen_lin + price_level[:, None] + gen_part
        gen_next = jnp.clip(gen_mid - TAU * gen_grad, 0.0, gen_max)
        stor_grad = (
            2.0 * stor_quad * stor_mid
            + price_level[:, None]
            + stor_price
            + reverse_cum(dual_store, HOURS)
        )
        stor_next = jnp.clip(stor_mid - TAU * stor_grad, -stor_rate, stor_rate)
        gen_bar = 2.0 * gen_next - gen_now
        stor_bar = 2.0 * stor_next - stor_now
        balance_term = jnp.sum(gen_bar, axis=1) + jnp.sum(stor_bar, axis=1) - load_total
        stor_inject = jnp.zeros((row_count, bus_count), jnp.float32).at[:, stor_bus].add(stor_bar)
        slotted = jnp.zeros((gen_bar.shape[0], slot_width), jnp.float32).at[:, column].set(gen_bar)
        received = lax.all_to_all(
            slotted.astype(jnp.bfloat16), "buses", split_axis=1, concat_axis=1, tiled=True
        ).astype(slotted.dtype)
        empty = jnp.zeros((received.shape[0], bus_count), jnp.float32)
        injection = empty.at[:, arrived_bus].add(received) + stor_inject - load
        inj_low = injection.astype(jnp.bfloat16)
        flow_share = lax.psum_scatter(
            lax.dot_general(
                ptdf, inj_low, (((1,), (1,)), ((), ())), preferred_element_type=jnp.float32
            ),
            "buses",
            scatter_dimension=0,
            tiled=True,
        ).T
        balance = lax.psum(balance_term, "buses")
        dual_flow = dual_step(dual_flow, flow_share, SIGMA_FLOW, -limit_share, limit_share)
        price_level = price_level + KAPPA / total_units * balance
        dual_store = dual_step(
            dual_store, forward_cum(stor_bar, HOURS), SIGMA_STORE, low_bound, high_bound
        )
        gen_old, stor_old = (gen_now, stor_now)
        gen_now, stor_now = (gen_next, stor_next)
    return (gen_now, stor_now, price_level, dual_flow, dual_store)


def solution(mesh):
    return jax.shard_map(
        shards,
        mesh=mesh,
        in_specs=(
            P("lines", "buses"),
            P(None, "buses"),
            P(),
            P("lines"),
            P("buses"),
            P("buses"),
            P("buses"),
            P("buses"),
            P(None, "buses"),
            P("buses"),
            P("buses"),
            P("buses"),
            P("buses"),
            P(None, "buses"),
            P(),
            P(None, ("lines", "buses")),
            P(None, "buses"),
        ),
        out_specs=(
            P(None, "buses"),
            P(None, "buses"),
            P(),
            P(None, ("lines", "buses")),
            P(None, "buses"),
        ),
        check_vma=False,
    )
```

profile of v0, /device:TPU:0, one launch (start us, length us, event | category | flops | bytes accessed | tf_op | source)
XLA Modules:
  0.0 342.7 jit_solution(5107921957427476958)
XLA Ops:
  9.0 1.4 scatter_custom_fusion
  11.1 6.4 %all-to-all-start = ((s32[1,8,32]{2,0,1:T(1,128)}), s32[1,8,32]{2,0,1:T(1,128)S(1)}, u32[]{:S(2)}, u32[]{:S(2)}) async-start(s32[1,8,32]{2,0,1:T(1,128)} %all_to_all.30), calls=%async_computation | async-start | bytes 8192 | tf_op jit(solution)/shard_map/all_to_all | solution.py:68
  18.4 15.0 %all_gather.6 = bf16[384,1024]{1,0:T(8,128)(2,1)S(1)} all-gather(bf16[384,128]{1,0:T(8,128)(2,1)S(1)} %convert_element_type.65), channel_id=1, replica_groups=mesh['lines'=4,'buses'=8] {'buses'}, dimensions={1}, use_global_device_ids=true | all-gather | bytes 884736 | tf_op jit(solution)/shard_map/all_gather | solution.py:89
  33.4 2.2 convolution_convert_fusion.1
  35.7 1.2 fusion.57
  37.1 50.5 %all-reduce.3.cloned.1.call-done = bf16[384,1280]{1,0:T(8,128)(2,1)} async-done(((bf16[384,1280]{1,0:T(8,128)(2,1)}), bf16[384,1280]{1,0:T(8,128)(2,1)}) %all-reduce.3.cloned.1.call-update) | async-done | bytes 983056 | tf_op jit(solution)/shard_map/psum | solution.py:91
  87.7 2.5 copy.69
  90.2 2.7 gather_fusion.1
  93.7 4.6 %all-to-all-start.1 = ((bf16[384,8,32]{0,2,1:T(8,128)(2,1)}), bf16[384,8,32]{0,2,1:T(8,128)(2,1)}, u32[]{:S(2)}, u32[]{:S(2)}) async-start(bf16[384,8,32]{0,2,1:T(8,128)(2,1)} %bitcast.4), calls=%async_computation.1 | async-start | bytes 393216 | tf_op jit(solution)/shard_map/all_to_all | solution.py:93
  98.3 1.2 copy.70
  100.8 2.9 copy.78
  103.8 3.0 all-to-all-done.1
  107.7 1.7 gather_fusion.2
  109.4 1.8 fusion.36
  111.3 2.2 scatter_custom_fusion.1
  113.4 1.7 convert_element_type.72
  115.1 4.0 %all-to-all-start.2 = ((bf16[384,8,32]{0,2,1:T(8,128)(2,1)}), bf16[384,8,32]{0,2,1:T(8,128)(2,1)}, u32[]{:S(2)}, u32[]{:S(2)}) async-start(bf16[384,8,32]{0,2,1:T(8,128)(2,1)} %bitcast.136), calls=%async_computation.2 | async-start | bytes 393216 | tf_op jit(solution)/shard_map/all_to_all | solution.py:118
  119.9 3.1 gather_fusion.3
  122.9 1.7 copy.74
  124.7 2.5 fusion.53
  127.5 1.7 bitcast_convert_fusion.4
  129.2 4.7 %scatter_custom_fusion.2 = f32[384,1280]{0,1:T(8,128)} fusion(s32[384]{0:T(512)} %add_reduce_fusion, f32[]{:T(128)} %constant.64.clone.1, f32[384,128]{0,1:T(8,128)S(1)} %copy.77, f32[]{:T(128)} %constant.140, f32[384,256]{0,1:T(8,128)} %bitcast_convert_fusion.4), kind=kCustom, calls=%fused_computation.22 | custom fusion | flops 294912 | bytes 2556928 | tf_op jit(solution)/shard_map/add | solution.py:122
  133.8 4.5 %convolution_bitcast_fusion.1 = f32[1024,384]{0,1:T(8,128)} fusion(bf16[1024,1280]{1,0:T(8,128)(2,1)S(1)} %copy-done, f32[384,1280]{0,1:T(8,128)} %scatter_custom_fusion.2, f32[384,1280]{0,1:T(8,128)} %copy.78), kind=kOutput, calls=%fused_computation.17 | convolution fusion | flops 1007616000 | bytes 8126464 | tf_op jit(solution)/shard_map/dot_general | solution.py:125
  139.3 6.1 %gather_fusion = f32[1024]{0:T(1024)S(1)} fusion(f32[32768]{0:T(1024)S(1)} %copy-done.1, s32[1024]{0:T(1024)S(1)} %fusion.41), kind=kCustom, calls=%fused_computation.6 | custom fusion | bytes 12288 | tf_op jit(solution)/shard_map/jit(_take)/gather | solution.py:70
  145.5 27.4 %reduce-scatter.3.cloned.1.call-done = f32[128,384]{0,1:T(8,128)} async-done(((f32[1024,384]{0,1:T(8,128)}), f32[128,384]{0,1:T(8,128)}) %reduce-scatter.3.cloned.1.call-update) | async-done | bytes 196624 | tf_op jit(solution)/shard_map/reduce_scatter | solution.py:124
  173.9 15.2 %all_gather.7 = bf16[384,1024]{1,0:T(8,128)(2,1)S(1)} all-gather(bf16[384,128]{1,0:T(8,128)(2,1)S(1)} %fusion.38), channel_id=1, replica_groups=mesh['lines'=4,'buses'=8] {'buses'}, dimensions={1}, use_global_device_ids=true | all-gather | bytes 884736 | tf_op jit(solution)/shard_map/all_gather | solution.py:89
  189.1 2.2 convolution_convert_fusion
  191.3 1.7 reduce_sum.57
  193.2 1.1 fusion.21
  195.7 45.8 %all-reduce.5.cloned.1.call-done = bf16[384,1280]{1,0:T(8,128)(2,1)} async-done(((bf16[384,1280]{1,0:T(8,128)(2,1)}), bf16[384,1280]{1,0:T(8,128)(2,1)}) %all-reduce.5.cloned.1.call-update) | async-done | bytes 983056 | tf_op jit(solution)/shard_map/psum | solution.py:91
  241.5 2.5 copy.79
  244.0 2.8 gather_fusion.4
  247.7 4.6 %all-to-all-start.3 = ((bf16[384,8,32]{0,2,1:T(8,128)(2,1)}), bf16[384,8,32]{0,2,1:T(8,128)(2,1)}, u32[]{:S(2)}, u32[]{:S(2)}) async-start(bf16[384,8,32]{0,2,1:T(8,128)(2,1)} %bitcast.18), calls=%async_computation.4 | async-start | bytes 393216 | tf_op jit(solution)/shard_map/all_to_all | solution.py:93
  252.3 17.1 %psum.29 = f32[384]{0:T(512)S(1)} all-reduce(f32[384]{0:T(512)S(1)} %add_subtract_fusion.1), channel_id=1, replica_groups=mesh['lines'=4,'buses'=8] {'buses'}, use_global_device_ids=true, to_apply=%region_9.13 | all-reduce | flops 384 | bytes 3072 | tf_op jit(solution)/shard_map/psum | solution.py:132
  270.4 1.9 gather_fusion.5
  272.3 1.4 fusion.37
  273.7 2.0 scatter_custom_fusion.3
  276.4 4.2 %all-to-all-start.4 = ((bf16[384,8,32]{0,2,1:T(8,128)(2,1)}), bf16[384,8,32]{0,2,1:T(8,128)(2,1)}, u32[]{:S(2)}, u32[]{:S(2)}) async-start(bf16[384,8,32]{0,2,1:T(8,128)(2,1)} %bitcast.135), calls=%async_computation.5 | async-start | bytes 393216 | tf_op jit(solution)/shard_map/all_to_all | solution.py:118
  282.3 1.0 copy.85
  283.3 2.5 gather_fusion.6
  286.6 2.0 fusion.50
  288.9 1.7 bitcast_convert_fusion.2
  290.6 4.7 %scatter_custom_fusion.4 = f32[384,1280]{0,1:T(8,128)} fusion(s32[384]{0:T(512)} %add_reduce_fusion, f32[]{:T(128)} %constant.64.clone.1, f32[384,128]{0,1:T(8,128)S(1)} %copy.86, f32[]{:T(128)} %constant.140, f32[384,256]{0,1:T(8,128)} %bitcast_convert_fusion.2), kind=kCustom, calls=%fused_computation.20 | custom fusion | flops 294912 | bytes 2556928 | tf_op jit(solution)/shard_map/add | solution.py:122
  295.3 4.5 %convolution_bitcast_fusion = f32[1024,384]{0,1:T(8,128)} fusion(bf16[1024,1280]{1,0:T(8,128)(2,1)S(1)} %copy-done, f32[384,1280]{0,1:T(8,128)} %scatter_custom_fusion.4, f32[384,1280]{0,1:T(8,128)} %copy.78), kind=kOutput, calls=%fused_computation.16 | convolution fusion | flops 1007616000 | bytes 8126464 | tf_op jit(solution)/shard_map/dot_general | solution.py:125
  300.5 1.7 fusion.23
  303.2 16.8 %psum.31 = f32[384]{0:T(512)S(1)} all-reduce(f32[384]{0:T(512)S(1)} %add_subtract_fusion), channel_id=1, replica_groups=mesh['lines'=4,'buses'=8] {'buses'}, use_global_device_ids=true, to_apply=%region_18.22 | all-reduce | flops 384 | bytes 3072 | tf_op jit(solution)/shard_map/psum | solution.py:132
  320.6 13.8 %reduce-scatter.5.cloned.1.call-done = f32[128,384]{0,1:T(8,128)} async-done(((f32[1024,384]{0,1:T(8,128)}), f32[128,384]{0,1:T(8,128)}) %reduce-scatter.5.cloned.1.call-update) | async-done | bytes 196624 | tf_op jit(solution)/shard_map/reduce_scatter | solution.py:124
  334.4 1.8 multiply_subtract_fusion.2
  (150 shorter events, 18.7 us)
Async XLA Ops:
  7.2 26.3 %copy-start = (bf16[1024,1280]{1,0:T(8,128)(2,1)S(1)}, bf16[1024,1280]{1,0:T(8,128)(2,1)}, u32[]{:S(2)}) copy-start(bf16[1024,1280]{1,0:T(8,128)(2,1)} %param.23) | copy-start | bytes 7864324
  9.0 100.4 %copy-start.16 = (pred[256]{0:T(512)(128)(4,1)}, pred[256]{0:T(512)(128)(4,1)S(1)}, u32[]{:S(2)}) copy-start(pred[256]{0:T(512)(128)(4,1)S(1)} %get-tuple-element.33) | copy-start | bytes 772
  9.0 102.3 %copy-start.22 = (s32[256]{0:T(256)}, s32[256]{0:T(256)S(1)}, u32[]{:S(2)}) copy-start(s32[256]{0:T(256)S(1)} %get-tuple-element.34) | copy-start | bytes 3076
  11.1 25.9 %all-to-all-start = ((s32[1,8,32]{2,0,1:T(1,128)}), s32[1,8,32]{2,0,1:T(1,128)S(1)}, u32[]{:S(2)}, u32[]{:S(2)}) async-start(s32[1,8,32]{2,0,1:T(1,128)} %all_to_all.30), calls=%async_computation | async-start | bytes 8192 | tf_op jit(solution)/shard_map/all_to_all | solution.py:68
  17.4 70.2 %all-reduce.3.cloned.1.call-start = ((), (), s32[]{:S(2)}) async-start(), calls=%async_computation.7 | async-start | bytes 1966080 | tf_op jit(solution)/shard_map/psum | solution.py:91
  33.4 2.2 copy-start.6
  35.6 1.3 copy-start.39
  37.0 87.7 %copy-start.25 = (pred[128]{0:T(512)(128)(4,1)}, pred[128]{0:T(512)(128)(4,1)S(1)}, u32[]{:S(2)}) copy-start(pred[128]{0:T(512)(128)(4,1)S(1)} %get-tuple-element.35) | copy-start | bytes 388
  37.1 55.8 %copy-start.11 = (s32[1024]{0:T(1024)}, s32[1024]{0:T(1024)S(1)}, u32[]{:S(2)}) copy-start(s32[1024]{0:T(1024)S(1)} %pad_clamp_fusion.2) | copy-start | bytes 12292
  37.1 55.8 %copy-start.30 = (pred[256]{0:T(512)(128)(4,1)}, pred[256]{0:T(512)(128)(4,1)S(1)}, u32[]{:S(2)}) copy-start(pred[256]{0:T(512)(128)(4,1)S(1)} %compare_and_fusion.2) | copy-start | bytes 772
  90.2 8.1 %copy-start.40 = (f32[128]{0:T(128)S(1)}, f32[128]{0:T(128)}, u32[]{:S(2)}) copy-start(f32[128]{0:T(128)} %param.33) | copy-start | bytes 1540
  90.2 9.3 %copy-start.23 = (f32[128]{0:T(128)S(1)}, f32[128]{0:T(128)}, u32[]{:S(2)}) copy-start(f32[128]{0:T(128)} %param.34) | copy-start | bytes 1540
  93.7 13.0 %all-to-all-start.1 = ((bf16[384,8,32]{0,2,1:T(8,128)(2,1)}), bf16[384,8,32]{0,2,1:T(8,128)(2,1)}, u32[]{:S(2)}, u32[]{:S(2)}) async-start(bf16[384,8,32]{0,2,1:T(8,128)(2,1)} %bitcast.4), calls=%async_computation.1 | async-start | bytes 393216 | tf_op jit(solution)/shard_map/all_to_all | solution.py:93
  98.3 26.4 %copy-start.27 = (f32[128]{0:T(128)}, f32[128]{0:T(128)S(1)}, u32[]{:S(2)}) copy-start(f32[128]{0:T(128)S(1)} %broadcast_multiply_fusion.2) | copy-start | bytes 1540
  100.8 2.9 copy-start.38
  103.7 5.7 %copy-start.12 = (s32[1024]{0:T(1024)}, s32[1024]{0:T(1024)S(1)}, u32[]{:S(2)}) copy-start(s32[1024]{0:T(1024)S(1)} %pad_clamp_fusion.1) | copy-start | bytes 12292
  103.7 5.7 %copy-start.9 = (f32[256]{0:T(256)}, f32[256]{0:T(256)S(1)}, u32[]{:S(2)}) copy-start(f32[256]{0:T(256)S(1)} %broadcast_multiply_fusion) | copy-start | bytes 3076
  103.7 5.7 %copy-start.7 = (f32[384]{0:T(512)S(1)}, f32[384]{0:T(512)}, u32[]{:S(2)}) copy-start(f32[384]{0:T(512)} %param.37) | copy-start | bytes 4612
  103.7 5.7 %copy-start.18 = (f32[256]{0:T(256)S(1)}, f32[256]{0:T(256)}, u32[]{:S(2)}) copy-start(f32[256]{0:T(256)} %param.29) | copy-start | bytes 3076
  103.8 5.7 %copy-start.20 = (f32[256]{0:T(256)S(1)}, f32[256]{0:T(256)}, u32[]{:S(2)}) copy-start(f32[256]{0:T(256)} %param.30) | copy-start | bytes 3076
  111.3 11.7 %copy-start.2 = (f32[384,256]{0,1:T(8,128)}, f32[384,256]{0,1:T(8,128)S(1)}, u32[]{:S(2)}) copy-start(f32[384,256]{0,1:T(8,128)S(1)} %get-tuple-element.32) | copy-start | bytes 1179652
  115.1 12.3 %all-to-all-start.2 = ((bf16[384,8,32]{0,2,1:T(8,128)(2,1)}), bf16[384,8,32]{0,2,1:T(8,128)(2,1)}, u32[]{:S(2)}, u32[]{:S(2)}) async-start(bf16[384,8,32]{0,2,1:T(8,128)(2,1)} %bitcast.136), calls=%async_computation.2 | async-start | bytes 393216 | tf_op jit(solution)/shard_map/all_to_all | solution.py:118
  119.2 53.8 %reduce-scatter.3.cloned.1.call-start = ((), (), s32[]{:S(2)}) async-start(), calls=%async_computation.8 | async-start | bytes 1769472 | tf_op jit(solution)/shard_map/reduce_scatter | solution.py:124
  119.2 5.4 %copy-start.15 = (s32[1024]{0:T(1024)}, s32[1024]{0:T(1024)S(1)}, u32[]{:S(2)}) copy-start(s32[1024]{0:T(1024)S(1)} %pad_clamp_fusion) | copy-start | bytes 12292
  133.8 4.6 %copy-start.8 = (s32[1024]{0:T(1024)S(1)}, s32[1024]{0:T(1024)}, u32[]{:S(2)}) copy-start(s32[1024]{0:T(1024)} %param.26) | copy-start | bytes 12292
  138.4 0.9 copy-start.1
  138.4 103.1 %all-reduce.5.cloned.1.call-start = ((), (), s32[]{:S(2)}) async-start(), calls=%async_computation.9 | async-start | bytes 1966080 | tf_op jit(solution)/shard_map/psum | solution.py:91
  139.3 33.7 %copy-start.3 = (f32[384,128]{1,0:T(8,128)S(1)}, f32[384,128]{1,0:T(8,128)}, u32[]{:S(2)}) copy-start(f32[384,128]{1,0:T(8,128)} %param.38) | copy-start | bytes 589828
  191.3 1.8 copy-start.41
  193.0 48.5 %copy-start.32 = (pred[384]{0:T(512)(128)(4,1)}, pred[384]{0:T(512)(128)(4,1)S(1)}, u32[]{:S(2)}) copy-start(pred[384]{0:T(512)(128)(4,1)S(1)} %fusion.42) | copy-start | bytes 1156
  193.1 1.9 copy-start.36
  193.1 48.5 %copy-start.34 = (f32[128]{0:T(128)}, f32[128]{0:T(128)S(1)}, u32[]{:S(2)}) copy-start(f32[128]{0:T(128)S(1)} %get-tuple-element.43) | copy-start | bytes 1540
  195.7 51.2 %copy-start.31 = (pred[256]{0:T(512)(128)(4,1)S(1)}, pred[256]{0:T(512)(128)(4,1)}, u32[]{:S(2)}) copy-start(pred[256]{0:T(512)(128)(4,1)} %copy-done.30) | copy-start | bytes 772
  244.0 8.2 %copy-start.13 = (f32[384]{0:T(512)S(1)}, f32[384]{0:T(512)}, u32[]{:S(2)}) copy-start(f32[384]{0:T(512)} %get-tuple-element.31) | copy-start | bytes 4612
  244.0 8.2 %copy-start.14 = (f32[384]{0:T(512)S(1)}, f32[384]{0:T(512)}, u32[]{:S(2)}) copy-start(f32[384]{0:T(512)} %get-tuple-element.28) | copy-start | bytes 4612
  247.7 21.8 %all-to-all-start.3 = ((bf16[384,8,32]{0,2,1:T(8,128)(2,1)}), bf16[384,8,32]{0,2,1:T(8,128)(2,1)}, u32[]{:S(2)}, u32[]{:S(2)}) async-start(bf16[384,8,32]{0,2,1:T(8,128)(2,1)} %bitcast.18), calls=%async_computation.4 | async-start | bytes 393216 | tf_op jit(solution)/shard_map/all_to_all | solution.py:93
  269.4 2.9 copy-start.10
  269.4 2.9 copy-start.17
  269.4 2.9 copy-start.19
  269.5 2.9 copy-start.21
  276.4 10.2 %copy-start.24 = (f32[128]{0:T(128)S(1)}, f32[128]{0:T(128)}, u32[]{:S(2)}) copy-start(f32[128]{0:T(128)} %param.34) | copy-start | bytes 1540
  276.4 10.2 %copy-start.26 = (pred[128]{0:T(512)(128)(4,1)S(1)}, pred[128]{0:T(512)(128)(4,1)}, u32[]{:S(2)}) copy-start(pred[128]{0:T(512)(128)(4,1)} %copy-done.25) | copy-start | bytes 388
  276.4 10.2 %copy-start.28 = (f32[128]{0:T(128)S(1)}, f32[128]{0:T(128)}, u32[]{:S(2)}) copy-start(f32[128]{0:T(128)} %copy-done.27) | copy-start | bytes 1540
  276.4 10.2 %copy-start.29 = (f32[128]{0:T(128)S(1)}, f32[128]{0:T(128)}, u32[]{:S(2)}) copy-start(f32[128]{0:T(128)} %neg.12) | copy-start | bytes 1540
  276.4 12.5 %all-to-all-start.4 = ((bf16[384,8,32]{0,2,1:T(8,128)(2,1)}), bf16[384,8,32]{0,2,1:T(8,128)(2,1)}, u32[]{:S(2)}, u32[]{:S(2)}) async-start(bf16[384,8,32]{0,2,1:T(8,128)(2,1)} %bitcast.135), calls=%async_computation.5 | async-start | bytes 393216 | tf_op jit(solution)/shard_map/all_to_all | solution.py:118
  280.6 53.8 %reduce-scatter.5.cloned.1.call-start = ((), (), s32[]{:S(2)}) async-start(), calls=%async_computation.10 | async-start | bytes 1769472 | tf_op jit(solution)/shard_map/reduce_scatter | solution.py:124
  299.8 0.7 copy-start.37
  299.8 34.6 %copy-start.4 = (f32[384,128]{1,0:T(8,128)S(1)}, f32[384,128]{1,0:T(8,128)}, u32[]{:S(2)}) copy-start(f32[384,128]{1,0:T(8,128)} %param.38) | copy-start | bytes 589828
  (3 other events, 2.0 us)
Sparse Core Ops, SparseCore 0:
  35.8 51.8 all-reduce.2
  138.5 34.3 reduce-scatter.2
  191.4 50.0 all-reduce.4
  300.0 34.3 reduce-scatter.4
where the time goes:
time: 344 us; the launch traced here: 343 us
  waiting for transfers between devices  141 us (41%)
  blocking collectives  64.1 us (19%)
  other arithmetic  44.4 us (13%)
  local copies, waits for them, and re-layouts  41.6 us (12%)
  starting transfers between devices  23.9 us (7%)
  between operations  14.3 us (4%)
  matrix products  13.4 us (4%)
    psum x2, waiting for transfers between devices, shards(): lax.psum(partial_value.astype(jnp.bfloat16), 'lines').astype(jnp.float32)  96.4 us
    reduce_scatter x2, waiting for transfers between devices, shards(): lax.psum_scatter(lax.dot_general(ptdf, inj_low, (((1,), (1,)), ((), ())),...  41.2 us
    psum x2, blocking collectives, shards(): balance = lax.psum(balance_term, 'buses')  34 us
    all_gather x2, blocking collectives, shards(): lax.all_gather(dual_flow.astype(jnp.bfloat16), 'buses', axis=1, tiled=True)  30.2 us
    add x2, other arithmetic, shards(): injection = empty.at[:, arrived_bus].add(received) + stor_inject - load  9.35 us
    all_to_all x2, starting transfers between devices, shards(): lax.all_to_all(jnp.take(bus_price, arrived_bus, axis=1).astype(jnp.bfloat...  9.21 us
    dot_general x2, matrix products, shards(): lax.dot_general(ptdf, inj_low, (((1,), (1,)), ((), ())), preferred_elemen...  9.06 us
    all_to_all x2, starting transfers between devices, shards(): lax.all_to_all(slotted.astype(jnp.bfloat16), 'buses', split_axis=1, conca...  8.18 us
  transfers between devices with their start and end apart: 9, of which 7 were waited for; matrix products, arithmetic and copies ran while one was open for 11% of the time, Pallas kernels for 0%

commit v1 on v0

--- a/solution.py
+++ b/solution.py
@@ -129,7 +129,10 @@
             scatter_dimension=0,
             tiled=True,
         ).T
-        balance = lax.psum(balance_term, "buses")
+        count, balance = (lax.axis_size("buses"), balance_term)
+        for far in [1 << k for k in range(count.bit_length() - 1)]:
+            pairs = [(i, i ^ far) for i in range(count)]
+            balance = balance + lax.ppermute(balance, "buses", pairs)
         dual_flow = dual_step(dual_flow, flow_share, SIGMA_FLOW, -limit_share, limit_share)
         price_level = price_level + KAPPA / total_units * balance
         dual_store = dual_step(

time: 344 us -> 336 us (0.977)
  blocking collectives: 64.1 us -> 30.2 us
  waiting for transfers between devices: 141 us -> 159 us
  starting transfers between devices: 23.9 us -> 29.6 us
    psum x2 -> x0, blocking collectives: 34 us -> none  [shards(): balance = lax.psum(balance_term, 'buses')]
    reduce_scatter x2, waiting for transfers between devices: 41.2 us -> 51.5 us  [shards(): lax.psum_scatter(lax.dot_general(ptdf, inj_low, (((1,), (1,)), ((), ())),...]
    ppermute x0 -> x6, waiting for transfers between devices: none -> 5.93 us  [shards(): balance = balance + lax.ppermute(balance, 'buses', pairs)]
    all_to_all x2, waiting for transfers between devices: 2.96 us -> 8.79 us  [shards(): lax.all_to_all(jnp.take(bus_price, arrived_bus, axis=1).astype(jnp.bfloat...]
    ppermute x0 -> x6, starting transfers between devices: none -> 5.73 us  [shards(): balance = balance + lax.ppermute(balance, 'buses', pairs)]
    psum x2, waiting for transfers between devices: 96.4 us -> 92.8 us  [shards(): lax.psum(partial_value.astype(jnp.bfloat16), 'lines').astype(jnp.float32)]
    unnamed x87 -> x83, local copies, waits for them, and re-layouts: 7.12 us -> 6.62 us
  transfers between devices with their start and end apart: 9 -> 15, of which waited for: 7 -> 12; matrix products, arithmetic and copies ran while one was open for 11% -> 14% of each run, Pallas kernels for 0% -> 0%
where the time goes in v1:
time: 336 us; the launch traced here: 334 us
  waiting for transfers between devices  159 us (47%)
  other arithmetic  45.4 us (14%)
  local copies, waits for them, and re-layouts  41.8 us (12%)
  blocking collectives  30.2 us (9%)
  starting transfers between devices  29.6 us (9%)
  between operations  14.3 us (4%)
  matrix products  13.4 us (4%)
    psum x2, waiting for transfers between devices, shards(): lax.psum(partial_value.astype(jnp.bfloat16), 'lines').astype(jnp.float32)  92.8 us
    reduce_scatter x2, waiting for transfers between devices, shards(): lax.psum_scatter(lax.dot_general(ptdf, inj_low, (((1,), (1,)), ((), ())),...  51.5 us
    all_gather x2, blocking collectives, shards(): lax.all_gather(dual_flow.astype(jnp.bfloat16), 'buses', axis=1, tiled=True)  30.2 us
    add x2, other arithmetic, shards(): injection = empty.at[:, arrived_bus].add(received) + stor_inject - load  9.32 us
    all_to_all x2, starting transfers between devices, shards(): lax.all_to_all(jnp.take(bus_price, arrived_bus, axis=1).astype(jnp.bfloat...  9.21 us
    dot_general x2, matrix products, shards(): lax.dot_general(ptdf, inj_low, (((1,), (1,)), ((), ())), preferred_elemen...  9.1 us
    all_to_all x2, waiting for transfers between devices, shards(): lax.all_to_all(jnp.take(bus_price, arrived_bus, axis=1).astype(jnp.bfloat...  8.79 us
    all_to_all x2, starting transfers between devices, shards(): lax.all_to_all(slotted.astype(jnp.bfloat16), 'buses', split_axis=1, conca...  8.18 us
  transfers between devices with their start and end apart: 15, of which 12 were waited for; matrix products, arithmetic and copies ran while one was open for 14% of the time, Pallas kernels for 0%

profile of v1, /device:TPU:0, one launch (start us, length us, event | category | flops | bytes accessed | tf_op | source)
XLA Modules:
  0.0 334.2 jit_solution(662771394135945724)
XLA Ops:
  9.0 1.4 scatter_custom_fusion
  11.1 6.4 %all-to-all-start = ((s32[1,8,32]{2,0,1:T(1,128)}), s32[1,8,32]{2,0,1:T(1,128)S(1)}, u32[]{:S(2)}, u32[]{:S(2)}) async-start(s32[1,8,32]{2,0,1:T(1,128)} %all_to_all.30), calls=%async_computation | async-start | bytes 8192 | tf_op jit(solution)/shard_map/all_to_all | solution.py:68
  18.4 15.0 %all_gather.6 = bf16[384,1024]{1,0:T(8,128)(2,1)S(1)} all-gather(bf16[384,128]{1,0:T(8,128)(2,1)S(1)} %convert_element_type.65), channel_id=1, replica_groups=mesh['lines'=4,'buses'=8] {'buses'}, dimensions={1}, use_global_device_ids=true | all-gather | bytes 884736 | tf_op jit(solution)/shard_map/all_gather | solution.py:89
  33.4 2.2 convolution_convert_fusion.1
  35.7 1.2 fusion.57
  37.1 50.5 %all-reduce.3.cloned.1.call-done = bf16[384,1280]{1,0:T(8,128)(2,1)} async-done(((bf16[384,1280]{1,0:T(8,128)(2,1)}), bf16[384,1280]{1,0:T(8,128)(2,1)}) %all-reduce.3.cloned.1.call-update) | async-done | bytes 983056 | tf_op jit(solution)/shard_map/psum | solution.py:91
  87.7 2.5 copy.69
  90.2 2.7 gather_fusion.1
  93.7 4.6 %all-to-all-start.1 = ((bf16[384,8,32]{0,2,1:T(8,128)(2,1)}), bf16[384,8,32]{0,2,1:T(8,128)(2,1)}, u32[]{:S(2)}, u32[]{:S(2)}) async-start(bf16[384,8,32]{0,2,1:T(8,128)(2,1)} %bitcast.4), calls=%async_computation.1 | async-start | bytes 393216 | tf_op jit(solution)/shard_map/all_to_all | solution.py:93
  100.8 2.9 copy.78
  103.8 2.9 all-to-all-done.1
  107.7 1.7 gather_fusion.2
  109.4 1.8 fusion.36
  111.3 2.2 scatter_custom_fusion.1
  113.4 1.7 convert_element_type.72
  115.2 4.0 %all-to-all-start.2 = ((bf16[384,8,32]{0,2,1:T(8,128)(2,1)}), bf16[384,8,32]{0,2,1:T(8,128)(2,1)}, u32[]{:S(2)}, u32[]{:S(2)}) async-start(bf16[384,8,32]{0,2,1:T(8,128)(2,1)} %bitcast.136), calls=%async_computation.2 | async-start | bytes 393216 | tf_op jit(solution)/shard_map/all_to_all | solution.py:118
  119.9 3.1 gather_fusion.3
  123.0 1.7 copy.74
  124.7 2.5 fusion.53
  127.5 1.7 bitcast_convert_fusion.4
  129.2 4.7 %scatter_custom_fusion.2 = f32[384,1280]{0,1:T(8,128)} fusion(s32[384]{0:T(512)} %add_reduce_fusion, f32[]{:T(128)} %constant.64.clone.1, f32[384,128]{0,1:T(8,128)S(1)} %copy.77, f32[]{:T(128)} %constant.140, f32[384,256]{0,1:T(8,128)} %bitcast_convert_fusion.4), kind=kCustom, calls=%fused_computation.22 | custom fusion | flops 294912 | bytes 2556928 | tf_op jit(solution)/shard_map/add | solution.py:122
  133.8 4.6 %convolution_bitcast_fusion.1 = f32[1024,384]{0,1:T(8,128)} fusion(bf16[1024,1280]{1,0:T(8,128)(2,1)S(1)} %copy-done, f32[384,1280]{0,1:T(8,128)} %scatter_custom_fusion.2, f32[384,1280]{0,1:T(8,128)} %copy.78), kind=kOutput, calls=%fused_computation.17 | convolution fusion | flops 1007616000 | bytes 8126464 | tf_op jit(solution)/shard_map/dot_general | solution.py:125
  139.3 6.1 %gather_fusion = f32[1024]{0:T(1024)S(1)} fusion(f32[32768]{0:T(1024)S(1)} %copy-done.1, s32[1024]{0:T(1024)S(1)} %fusion.41), kind=kCustom, calls=%fused_computation.6 | custom fusion | bytes 12288 | tf_op jit(solution)/shard_map/jit(_take)/gather | solution.py:70
  145.6 27.5 %reduce-scatter.3.cloned.1.call-done = f32[128,384]{0,1:T(8,128)} async-done(((f32[1024,384]{0,1:T(8,128)}), f32[128,384]{0,1:T(8,128)}) %reduce-scatter.3.cloned.1.call-update) | async-done | bytes 196624 | tf_op jit(solution)/shard_map/reduce_scatter | solution.py:124
  174.0 15.2 %all_gather.7 = bf16[384,1024]{1,0:T(8,128)(2,1)S(1)} all-gather(bf16[384,128]{1,0:T(8,128)(2,1)S(1)} %fusion.38), channel_id=1, replica_groups=mesh['lines'=4,'buses'=8] {'buses'}, dimensions={1}, use_global_device_ids=true | all-gather | bytes 884736 | tf_op jit(solution)/shard_map/all_gather | solution.py:89
  189.2 2.2 convolution_convert_fusion
  191.4 1.7 reduce_sum.57
  195.7 2.8 collective-permute-done.1
  199.4 42.3 %all-reduce.5.cloned.1.call-done = bf16[384,1280]{1,0:T(8,128)(2,1)} async-done(((bf16[384,1280]{1,0:T(8,128)(2,1)}), bf16[384,1280]{1,0:T(8,128)(2,1)}) %all-reduce.5.cloned.1.call-update) | async-done | bytes 983056 | tf_op jit(solution)/shard_map/psum | solution.py:91
  241.6 2.5 copy.79
  244.1 2.9 gather_fusion.4
  247.8 4.6 %all-to-all-start.3 = ((bf16[384,8,32]{0,2,1:T(8,128)(2,1)}), bf16[384,8,32]{0,2,1:T(8,128)(2,1)}, u32[]{:S(2)}, u32[]{:S(2)}) async-start(bf16[384,8,32]{0,2,1:T(8,128)(2,1)} %bitcast.18), calls=%async_computation.4 | async-start | bytes 393216 | tf_op jit(solution)/shard_map/all_to_all | solution.py:93
  255.0 5.8 %all-to-all-done.3 = bf16[384,8,32]{0,2,1:T(8,128)(2,1)} async-done(((bf16[384,8,32]{0,2,1:T(8,128)(2,1)}), bf16[384,8,32]{0,2,1:T(8,128)(2,1)}, u32[]{:S(2)}, u32[]{:S(2)}) %all-to-all-start.3) | async-done | bytes 196640 | tf_op jit(solution)/shard_map/all_to_all | solution.py:93
  261.8 1.9 gather_fusion.5
  263.6 1.4 fusion.37
  265.0 2.0 scatter_custom_fusion.3
  267.8 4.2 %all-to-all-start.4 = ((bf16[384,8,32]{0,2,1:T(8,128)(2,1)}), bf16[384,8,32]{0,2,1:T(8,128)(2,1)}, u32[]{:S(2)}, u32[]{:S(2)}) async-start(bf16[384,8,32]{0,2,1:T(8,128)(2,1)} %bitcast.135), calls=%async_computation.5 | async-start | bytes 393216 | tf_op jit(solution)/shard_map/all_to_all | solution.py:118
  274.6 2.5 gather_fusion.6
  278.0 2.0 fusion.50
  280.2 1.7 bitcast_convert_fusion.2
  281.9 4.7 %scatter_custom_fusion.4 = f32[384,1280]{0,1:T(8,128)} fusion(s32[384]{0:T(512)} %add_reduce_fusion, f32[]{:T(128)} %constant.64.clone.1, f32[384,128]{0,1:T(8,128)S(1)} %copy.86, f32[]{:T(128)} %constant.140, f32[384,256]{0,1:T(8,128)} %bitcast_convert_fusion.2), kind=kCustom, calls=%fused_computation.20 | custom fusion | flops 294912 | bytes 2556928 | tf_op jit(solution)/shard_map/add | solution.py:122
  286.6 4.5 %convolution_bitcast_fusion = f32[1024,384]{0,1:T(8,128)} fusion(bf16[1024,1280]{1,0:T(8,128)(2,1)S(1)} %copy-done, f32[384,1280]{0,1:T(8,128)} %scatter_custom_fusion.4, f32[384,1280]{0,1:T(8,128)} %copy.78), kind=kOutput, calls=%fused_computation.16 | convolution fusion | flops 1007616000 | bytes 8126464 | tf_op jit(solution)/shard_map/dot_general | solution.py:125
  292.4 1.7 collective-permute-start.4
  294.2 1.8 collective-permute-done.4
  296.0 2.6 collective-permute-start.5
  298.6 1.7 fusion.23
  301.8 24.0 %reduce-scatter.5.cloned.1.call-done = f32[128,384]{0,1:T(8,128)} async-done(((f32[1024,384]{0,1:T(8,128)}), f32[128,384]{0,1:T(8,128)}) %reduce-scatter.5.cloned.1.call-update) | async-done | bytes 196624 | tf_op jit(solution)/shard_map/reduce_scatter | solution.py:124
  325.8 1.8 multiply_subtract_fusion.2
  (160 shorter events, 25.9 us)
Async XLA Ops:
  7.2 26.3 %copy-start = (bf16[1024,1280]{1,0:T(8,128)(2,1)S(1)}, bf16[1024,1280]{1,0:T(8,128)(2,1)}, u32[]{:S(2)}) copy-start(bf16[1024,1280]{1,0:T(8,128)(2,1)} %param.23) | copy-start | bytes 7864324
  9.0 100.4 %copy-start.17 = (pred[256]{0:T(512)(128)(4,1)}, pred[256]{0:T(512)(128)(4,1)S(1)}, u32[]{:S(2)}) copy-start(pred[256]{0:T(512)(128)(4,1)S(1)} %get-tuple-element.33) | copy-start | bytes 772
  9.0 102.3 %copy-start.23 = (s32[256]{0:T(256)}, s32[256]{0:T(256)S(1)}, u32[]{:S(2)}) copy-start(s32[256]{0:T(256)S(1)} %get-tuple-element.34) | copy-start | bytes 3076
  11.1 25.9 %all-to-all-start = ((s32[1,8,32]{2,0,1:T(1,128)}), s32[1,8,32]{2,0,1:T(1,128)S(1)}, u32[]{:S(2)}, u32[]{:S(2)}) async-start(s32[1,8,32]{2,0,1:T(1,128)} %all_to_all.30), calls=%async_computation | async-start | bytes 8192 | tf_op jit(solution)/shard_map/all_to_all | solution.py:68
  17.4 70.2 %all-reduce.3.cloned.1.call-start = ((), (), s32[]{:S(2)}) async-start(), calls=%async_computation.7 | async-start | bytes 1966080 | tf_op jit(solution)/shard_map/psum | solution.py:91
  37.0 87.7 %copy-start.26 = (pred[128]{0:T(512)(128)(4,1)}, pred[128]{0:T(512)(128)(4,1)S(1)}, u32[]{:S(2)}) copy-start(pred[128]{0:T(512)(128)(4,1)S(1)} %get-tuple-element.35) | copy-start | bytes 388
  37.1 55.8 %copy-start.12 = (s32[1024]{0:T(1024)}, s32[1024]{0:T(1024)S(1)}, u32[]{:S(2)}) copy-start(s32[1024]{0:T(1024)S(1)} %pad_clamp_fusion.2) | copy-start | bytes 12292
  37.1 55.8 %copy-start.31 = (pred[256]{0:T(512)(128)(4,1)}, pred[256]{0:T(512)(128)(4,1)S(1)}, u32[]{:S(2)}) copy-start(pred[256]{0:T(512)(128)(4,1)S(1)} %compare_and_fusion.2) | copy-start | bytes 772
  90.2 8.1 %copy-start.38 = (f32[128]{0:T(128)S(1)}, f32[128]{0:T(128)}, u32[]{:S(2)}) copy-start(f32[128]{0:T(128)} %param.33) | copy-start | bytes 1540
  90.2 9.3 %copy-start.24 = (f32[128]{0:T(128)S(1)}, f32[128]{0:T(128)}, u32[]{:S(2)}) copy-start(f32[128]{0:T(128)} %param.34) | copy-start | bytes 1540
  93.7 13.0 %all-to-all-start.1 = ((bf16[384,8,32]{0,2,1:T(8,128)(2,1)}), bf16[384,8,32]{0,2,1:T(8,128)(2,1)}, u32[]{:S(2)}, u32[]{:S(2)}) async-start(bf16[384,8,32]{0,2,1:T(8,128)(2,1)} %bitcast.4), calls=%async_computation.1 | async-start | bytes 393216 | tf_op jit(solution)/shard_map/all_to_all | solution.py:93
  98.3 26.4 %copy-start.28 = (f32[128]{0:T(128)}, f32[128]{0:T(128)S(1)}, u32[]{:S(2)}) copy-start(f32[128]{0:T(128)S(1)} %broadcast_multiply_fusion.2) | copy-start | bytes 1540
  100.8 2.9 copy-start.36
  103.7 5.7 %copy-start.13 = (s32[1024]{0:T(1024)}, s32[1024]{0:T(1024)S(1)}, u32[]{:S(2)}) copy-start(s32[1024]{0:T(1024)S(1)} %pad_clamp_fusion.1) | copy-start | bytes 12292
  103.7 5.7 %copy-start.10 = (f32[256]{0:T(256)}, f32[256]{0:T(256)S(1)}, u32[]{:S(2)}) copy-start(f32[256]{0:T(256)S(1)} %broadcast_multiply_fusion) | copy-start | bytes 3076
  103.7 5.7 %copy-start.8 = (f32[384]{0:T(512)S(1)}, f32[384]{0:T(512)}, u32[]{:S(2)}) copy-start(f32[384]{0:T(512)} %param.37) | copy-start | bytes 4612
  103.8 5.7 %copy-start.19 = (f32[256]{0:T(256)S(1)}, f32[256]{0:T(256)}, u32[]{:S(2)}) copy-start(f32[256]{0:T(256)} %param.29) | copy-start | bytes 3076
  103.8 5.7 %copy-start.21 = (f32[256]{0:T(256)S(1)}, f32[256]{0:T(256)}, u32[]{:S(2)}) copy-start(f32[256]{0:T(256)} %param.30) | copy-start | bytes 3076
  111.3 11.7 %copy-start.2 = (f32[384,256]{0,1:T(8,128)}, f32[384,256]{0,1:T(8,128)S(1)}, u32[]{:S(2)}) copy-start(f32[384,256]{0,1:T(8,128)S(1)} %get-tuple-element.32) | copy-start | bytes 1179652
  115.2 12.3 %all-to-all-start.2 = ((bf16[384,8,32]{0,2,1:T(8,128)(2,1)}), bf16[384,8,32]{0,2,1:T(8,128)(2,1)}, u32[]{:S(2)}, u32[]{:S(2)}) async-start(bf16[384,8,32]{0,2,1:T(8,128)(2,1)} %bitcast.136), calls=%async_computation.2 | async-start | bytes 393216 | tf_op jit(solution)/shard_map/all_to_all | solution.py:118
  119.2 53.9 %reduce-scatter.3.cloned.1.call-start = ((), (), s32[]{:S(2)}) async-start(), calls=%async_computation.8 | async-start | bytes 1769472 | tf_op jit(solution)/shard_map/reduce_scatter | solution.py:124
  119.2 5.5 %copy-start.16 = (s32[1024]{0:T(1024)}, s32[1024]{0:T(1024)S(1)}, u32[]{:S(2)}) copy-start(s32[1024]{0:T(1024)S(1)} %pad_clamp_fusion) | copy-start | bytes 12292
  133.8 4.6 %copy-start.9 = (s32[1024]{0:T(1024)S(1)}, s32[1024]{0:T(1024)}, u32[]{:S(2)}) copy-start(s32[1024]{0:T(1024)} %param.26) | copy-start | bytes 12292
  138.4 103.2 %all-reduce.5.cloned.1.call-start = ((), (), s32[]{:S(2)}) async-start(), calls=%async_computation.9 | async-start | bytes 1966080 | tf_op jit(solution)/shard_map/psum | solution.py:91
  139.3 33.7 %copy-start.3 = (f32[384,128]{1,0:T(8,128)S(1)}, f32[384,128]{1,0:T(8,128)}, u32[]{:S(2)}) copy-start(f32[384,128]{1,0:T(8,128)} %param.38) | copy-start | bytes 589828
  193.7 1.2 collective-permute-start
  194.9 3.6 %collective-permute-start.1 = (f32[384]{0:T(512)S(1)}, f32[384]{0:T(512)S(1)}, u32[]{:S(2)}, u32[]{:S(2)}) collective-permute-start(f32[384]{0:T(512)S(1)} %add.218), channel_id=1, source_target_pairs={{0,2},{1,3},{2,0},{3,1},{4,6},{5,7},{6,4},{7,5},{8,10},{9,11},{10,... | collective-permute-start | bytes 4616 | tf_op jit(solution)/shard_map/ppermute | solution.py:135
  198.5 48.5 %copy-start.32 = (pred[256]{0:T(512)(128)(4,1)S(1)}, pred[256]{0:T(512)(128)(4,1)}, u32[]{:S(2)}) copy-start(pred[256]{0:T(512)(128)(4,1)} %copy-done.31) | copy-start | bytes 772
  198.5 56.4 %collective-permute-start.2 = (f32[384]{0:T(512)S(1)}, f32[384]{0:T(512)S(1)}, u32[]{:S(2)}, u32[]{:S(2)}) collective-permute-start(f32[384]{0:T(512)S(1)} %add.219), channel_id=1, source_target_pairs={{0,4},{1,5},{2,6},{3,7},{4,0},{5,1},{6,2},{7,3},{8,12},{9,13},{10,... | collective-permute-start | bytes 4616 | tf_op jit(solution)/shard_map/ppermute | solution.py:135
  244.1 8.3 %copy-start.7 = (f32[384,128]{1,0:T(8,128)S(1)}, f32[384,128]{1,0:T(8,128)}, u32[]{:S(2)}) copy-start(f32[384,128]{1,0:T(8,128)} %param.39) | copy-start | bytes 589828
  244.1 8.3 %copy-start.33 = (f32[128]{0:T(128)S(1)}, f32[128]{0:T(128)}, u32[]{:S(2)}) copy-start(f32[128]{0:T(128)} %get-tuple-element.43) | copy-start | bytes 1540
  244.1 8.3 %copy-start.34 = (f32[128]{0:T(128)S(1)}, f32[128]{0:T(128)}, u32[]{:S(2)}) copy-start(f32[128]{0:T(128)} %get-tuple-element.44) | copy-start | bytes 1540
  244.1 8.3 %copy-start.35 = (pred[384]{0:T(512)(128)(4,1)S(1)}, pred[384]{0:T(512)(128)(4,1)}, u32[]{:S(2)}) copy-start(pred[384]{0:T(512)(128)(4,1)} %fusion.42) | copy-start | bytes 1156
  247.8 13.0 %all-to-all-start.3 = ((bf16[384,8,32]{0,2,1:T(8,128)(2,1)}), bf16[384,8,32]{0,2,1:T(8,128)(2,1)}, u32[]{:S(2)}, u32[]{:S(2)}) async-start(bf16[384,8,32]{0,2,1:T(8,128)(2,1)} %bitcast.18), calls=%async_computation.4 | async-start | bytes 393216 | tf_op jit(solution)/shard_map/all_to_all | solution.py:93
  254.9 8.7 %copy-start.11 = (f32[256]{0:T(256)S(1)}, f32[256]{0:T(256)}, u32[]{:S(2)}) copy-start(f32[256]{0:T(256)} %copy-done.10) | copy-start | bytes 3076
  254.9 8.7 %copy-start.18 = (pred[256]{0:T(512)(128)(4,1)S(1)}, pred[256]{0:T(512)(128)(4,1)}, u32[]{:S(2)}) copy-start(pred[256]{0:T(512)(128)(4,1)} %copy-done.17) | copy-start | bytes 772
  254.9 8.7 %copy-start.20 = (f32[256]{0:T(256)S(1)}, f32[256]{0:T(256)}, u32[]{:S(2)}) copy-start(f32[256]{0:T(256)} %param.29) | copy-start | bytes 3076
  254.9 8.7 %copy-start.22 = (f32[256]{0:T(256)S(1)}, f32[256]{0:T(256)}, u32[]{:S(2)}) copy-start(f32[256]{0:T(256)} %param.30) | copy-start | bytes 3076
  267.7 10.2 %copy-start.25 = (f32[128]{0:T(128)S(1)}, f32[128]{0:T(128)}, u32[]{:S(2)}) copy-start(f32[128]{0:T(128)} %param.34) | copy-start | bytes 1540
  267.7 10.2 %copy-start.27 = (pred[128]{0:T(512)(128)(4,1)S(1)}, pred[128]{0:T(512)(128)(4,1)}, u32[]{:S(2)}) copy-start(pred[128]{0:T(512)(128)(4,1)} %copy-done.26) | copy-start | bytes 388
  267.7 10.2 %copy-start.29 = (f32[128]{0:T(128)S(1)}, f32[128]{0:T(128)}, u32[]{:S(2)}) copy-start(f32[128]{0:T(128)} %copy-done.28) | copy-start | bytes 1540
  267.8 10.2 %copy-start.30 = (f32[128]{0:T(128)S(1)}, f32[128]{0:T(128)}, u32[]{:S(2)}) copy-start(f32[128]{0:T(128)} %neg.12) | copy-start | bytes 1540
  267.8 12.5 %all-to-all-start.4 = ((bf16[384,8,32]{0,2,1:T(8,128)(2,1)}), bf16[384,8,32]{0,2,1:T(8,128)(2,1)}, u32[]{:S(2)}, u32[]{:S(2)}) async-start(bf16[384,8,32]{0,2,1:T(8,128)(2,1)} %bitcast.135), calls=%async_computation.5 | async-start | bytes 393216 | tf_op jit(solution)/shard_map/all_to_all | solution.py:118
  271.9 53.9 %reduce-scatter.5.cloned.1.call-start = ((), (), s32[]{:S(2)}) async-start(), calls=%async_computation.10 | async-start | bytes 1769472 | tf_op jit(solution)/shard_map/reduce_scatter | solution.py:124
  291.1 34.7 %copy-start.4 = (f32[384,128]{1,0:T(8,128)S(1)}, f32[384,128]{1,0:T(8,128)}, u32[]{:S(2)}) copy-start(f32[384,128]{1,0:T(8,128)} %param.38) | copy-start | bytes 589828
  291.2 1.2 collective-permute-start.3
  292.4 3.6 %collective-permute-start.4 = (f32[384]{0:T(512)S(1)}, f32[384]{0:T(512)S(1)}, u32[]{:S(2)}, u32[]{:S(2)}) collective-permute-start(f32[384]{0:T(512)S(1)} %add.239), channel_id=1, source_target_pairs={{0,2},{1,3},{2,0},{3,1},{4,6},{5,7},{6,4},{7,5},{8,10},{9,11},{10,... | collective-permute-start | bytes 4616 | tf_op jit(solution)/shard_map/ppermute | solution.py:135
  296.0 5.2 %collective-permute-start.5 = (f32[384]{0:T(512)S(1)}, f32[384]{0:T(512)S(1)}, u32[]{:S(2)}, u32[]{:S(2)}) collective-permute-start(f32[384]{0:T(512)S(1)} %add.240), channel_id=1, source_target_pairs={{0,4},{1,5},{2,6},{3,7},{4,0},{5,1},{6,2},{7,3},{8,12},{9,13},{10,... | collective-permute-start | bytes 4616 | tf_op jit(solution)/shard_map/ppermute | solution.py:135
  (7 other events, 11.5 us)
Sparse Core Ops, SparseCore 0:
  35.8 51.8 all-reduce.2
  138.5 34.4 reduce-scatter.2
  191.5 50.0 all-reduce.4
  291.3 34.4 reduce-scatter.4
